TPU v7x, 32 devices: a whole 2x2x4 slice. The times are simulated.
32 devices in a mesh: tm: 4 (over y, core), expert: 8 (over z, x).
Axes of the slice: x: 2, y: 2, z: 4, core: 2. Of those that a mesh axis runs over, the one named last changes fastest.
Arguments:
- queries: bfloat16 [4096, 2048], P(('tm', 'expert')), may hold values from -6 to 6
- keys: bfloat16 [4096, 2048], P(('tm', 'expert')), may hold values from -6 to 6
- values: bfloat16 [4096, 2048], P(('tm', 'expert')), may hold values from -6 to 6
- out_grad: bfloat16 [4096, 2048], P(('tm', 'expert')), may hold values from -6 to 6
- expert_ids: int32 [4096, 2], P(('tm', 'expert')), may hold values from 0 to 7, all different within a row
- combine_gates: float32 [4096, 2], P(('tm', 'expert')), may hold values from 0.2 to 1
- gate_weight: bfloat16 [32, 2048, 512], P(('tm', 'expert')), may hold values from -0.125 to 0.125
- up_weight: bfloat16 [32, 2048, 512], P(('tm', 'expert')), may hold values from -0.125 to 0.125
- down_weight: bfloat16 [32, 512, 2048], P(('tm', 'expert')), may hold values from -0.125 to 0.125
Outputs:
- query_grad: bfloat16 [4096, 2048], P(('tm', 'expert'))
- key_grad: bfloat16 [4096, 2048], P(('tm', 'expert'))
- value_grad: bfloat16 [4096, 2048], P(('tm', 'expert'))
- gate_weight_grad: float32 [32, 2048, 512], P(('tm', 'expert'))
- up_weight_grad: float32 [32, 2048, 512], P(('tm', 'expert'))
- down_weight_grad: float32 [32, 512, 2048], P(('tm', 'expert'))
Inputs may be any that keep to these rules, and one draw needn't show every extreme that they name: `expert_ids`: the two experts of a token differ.
All inputs are finite; a program needn't handle non-finite values.
Results may differ from a plain program's by a relative error of at most 0.017.
Values may be sent and summed in bfloat16 or wider, within the bound.
No kernel may reach another device: no remote copies, remote signals or barrier semaphores. Data moves between devices by JAX's collectives and lax.ppermute only.
A program may use at most 192 MiB of HBM per device.

v0:
```python
import functools

import jax
import jax.numpy as jnp
from jax import lax
from jax.experimental import pallas as pl
from jax.sharding import Mesh, PartitionSpec as P


HEAD_DIM = 128
SLICES = 4
EPSILON = 1e-06
ALL = ("tm", "eg", "sl")
F32 = jnp.float32
BF16 = jnp.bfloat16


def dot(a, b):
    return jnp.dot(a, b, preferred_element_type=F32)


def dot_nt(a, b):
    return lax.dot_general(a, b, (((1,), (1,)), ((), ())), preferred_element_type=F32)


def dot_tn(a, b):
    return lax.dot_general(a, b, (((0,), (0,)), ((), ())), preferred_element_type=F32)


def call(kernel, out_shape, *args, **options):
    return pl.pallas_call(kernel, out_shape=out_shape, **options)(*args)


def like(shape, dtype=BF16):
    return jax.ShapeDtypeStruct(shape, dtype)


def head_cols(h):
    return slice(h * HEAD_DIM, (h + 1) * HEAD_DIM)


def swap(value, bit):
    return lax.ppermute(value, "sl", [(i, i ^ bit) for i in range(SLICES)])


def exchange(value, axes):
    return lax.all_to_all(value, axes, split_axis=0, concat_axis=0, tiled=True)


def trade(blocks):
    count = len(blocks)
    moved = list(blocks)
    for k in range(1, count):
        moved[k] = lax.ppermute(blocks[k], ("tm", "eg"), [(i, i ^ k) for i in range(count)])
    return moved


def spread(rows, first):
    other = 3 - first
    one, two = swap(rows, first), swap(rows, other)
    far = swap(one, other)
    return {0: rows, first: one, other: two, 3: far}


def join_kernel(*refs):
    out = refs[-1]
    rows = refs[0].shape[0]
    for i, ref in enumerate(refs[:-1]):
        out[i * rows : (i + 1) * rows] = ref[...]


def join(blocks):
    rows, width = blocks[0].shape
    if rows % 16:
        return jnp.concatenate(blocks)
    return call(join_kernel, like((len(blocks) * rows, width)), *blocks)


def slot_places(routes, capacity, experts):
    flat_ids = routes.reshape(-1)
    onehot = (flat_ids[:, None] == jnp.arange(experts, dtype=jnp.int32)[None, :]).astype(jnp.int32)
    earlier = jnp.cumsum(onehot, axis=0) - onehot
    position = jnp.sum(earlier * onehot, axis=1)
    return jnp.where(position < capacity, flat_ids * capacity + position, experts * capacity)


def pick(places, choice, block, rows):
    slots = block * rows + lax.broadcasted_iota(jnp.int32, (rows, places.shape[1]), 0)
    return slots == places[choice : choice + 1]


def one_hot(mask):
    return jnp.where(mask, 1.0, 0.0).astype(BF16)


def outer_kernel(keys, values, out):
    for h in range(keys.shape[1] // HEAD_DIM):
        cols = head_cols(h)
        out[cols] = dot_tn(keys[:, cols], values[:, cols]).astype(BF16)


def slots_kernel(groups, sources, scaled, *refs):
    infos, tokens, outs = refs[:sources], refs[sources : 2 * sources], refs[2 * sources :]
    rows = outs[0].shape[0] // sources
    for n in range(sources):
        info = infos[n][...]
        spots = info[:2].astype(jnp.int32)
        blocks = []
        for q in range(len(outs)):
            picks = [pick(spots, k, q * groups, rows) for k in range(2)]
            if scaled:
                blocks.append(jnp.concatenate([one_hot(p) for p in picks], axis=1))
            else:
                blocks.append(one_hot(picks[0] | picks[1]))
        if scaled:
            grad = tokens[n][...].astype(F32)
            gates = info.T
            values = jnp.concatenate([(grad * gates[:, 2 + k : 3 + k]).astype(BF16) for k in range(2)])
        else:
            values = tokens[n][...]
        if rows % 16:
            for block, out in zip(blocks, outs):
                out[n * rows : (n + 1) * rows] = dot(block, values).astype(BF16)
        else:
            chosen = dot(jnp.concatenate(blocks), values).astype(BF16)
            for q, out in enumerate(outs):
                out[n * rows : (n + 1) * rows] = chosen[q * rows : (q + 1) * rows]


def slots(infos, tokens, capacity, times, groups, scaled):
    sources, width = len(tokens), tokens[0].shape[1]
    return call(
        functools.partial(slots_kernel, groups, sources, scaled),
        [like((sources * capacity, width))] * times,
        *infos, *tokens,
    )


def hidden_kernel(queries, states, hidden):
    for h in range(queries.shape[1] // HEAD_DIM):
        cols = head_cols(h)
        mixed = dot(queries[:, cols], states[cols])
        scale = lax.rsqrt(jnp.mean(mixed * mixed, axis=-1, keepdims=True) + EPSILON)
        hidden[:, cols] = (mixed * scale).astype(BF16)


def act_grad_kernel(*refs):
    ys, down_w, out = refs[:-2], refs[-2], refs[-1]
    out[...] = dot_nt(jnp.concatenate([y[...] for y in ys]), down_w[...])


def act_grads(ys, down_w):
    rows = sum(y.shape[0] for y in ys)
    return call(act_grad_kernel, like((rows, down_w.shape[0]), F32), *ys, down_w)


def expert_kernel(pieces, regroup, *refs):
    xs, (act_grad, gate_w, up_w, act_out, gg_out, ug_out), parts = refs[:pieces], refs[pieces : pieces + 6], refs[pieces + 6 :]
    x = jnp.concatenate([x[...] for x in xs])
    gate, upper, grad = dot(x, gate_w[...]), dot(x, up_w[...]), act_grad[...]
    sigma = jax.nn.sigmoid(gate)
    silu = gate * sigma
    act_out[...] = (silu * upper).astype(BF16)
    gg = (grad * upper * sigma * (1.0 + gate * (1.0 - sigma))).astype(BF16)
    ug = (grad * silu).astype(BF16)
    gg_out[...], ug_out[...] = gg, ug
    rows, width = parts[0].shape
    count = x.shape[0] // rows
    for j in range(len(parts) // count):
        cols = slice(j * width, (j + 1) * width)
        total = (dot_nt(gg, gate_w[cols]) + dot_nt(ug, up_w[cols])).astype(BF16)
        if regroup:
            block = rows // pieces
            for m in range(count):
                for q in range(pieces):
                    at = (q * count + m) * block
                    parts[count * j + m][q * block : (q + 1) * block] = total[at : at + block]
        else:
            for m in range(count):
                parts[count * j + m][...] = total[m * rows : (m + 1) * rows]


def expert_rows(xs, act_grad, gate_w, up_w, halves, count, regroup):
    total, width = sum(x.shape[0] for x in xs), xs[0].shape[1]
    hidden = gate_w.shape[1]
    outs = call(
        functools.partial(expert_kernel, len(xs), regroup),
        [like((total, hidden))] * 3 + [like((total // count, width // halves))] * (count * halves),
        *xs, act_grad, gate_w, up_w,
    )
    parts = [[outs[3 + count * j + m] for j in range(halves)] for m in range(count)]
    return outs[0], outs[1], outs[2], parts


def sum_kernel(count, *refs):
    total = refs[0][...].astype(F32)
    for ref in refs[1:count]:
        total = total + ref[...].astype(F32)
    outs = refs[count:]
    rows = outs[0].shape[0]
    if rows % 16 and len(outs) > 1:
        for n, out in enumerate(outs):
            part = refs[0][n * rows : (n + 1) * rows].astype(F32)
            for ref in refs[1:count]:
                part = part + ref[n * rows : (n + 1) * rows].astype(F32)
            out[...] = part.astype(BF16)
    else:
        total = total.astype(BF16)
        for n, out in enumerate(outs):
            out[...] = total[n * rows : (n + 1) * rows]


def add_up(pieces, count=1):
    rows, width = pieces[0].shape
    outs = call(functools.partial(sum_kernel, len(pieces)), [like((rows // count, width))] * count, *pieces)
    return outs[0] if count == 1 else outs


def wgrad_kernel(turned, count, *refs):
    rows, cols, out = refs[:count], refs[count:-1], refs[-1]
    left = jnp.concatenate([r[...] for r in rows])
    right = jnp.concatenate([c[...] for c in cols])
    out[...] = dot_tn(right, left) if turned else dot_tn(left, right)


def weight_grad(wide, narrow, turned):
    width, hidden = wide[0].shape[1], narrow[0].shape[1]
    block = min(1024, width)
    shape = (1, hidden, width) if turned else (1, width, hidden)
    out = (None, hidden, block) if turned else (None, block, hidden)
    return call(
        functools.partial(wgrad_kernel, turned, len(wide)),
        like(shape, F32),
        *wide, *narrow,
        grid=(width // block,),
        in_specs=[pl.BlockSpec((w.shape[0], block), lambda i: (0, i)) for w in wide]
        + [pl.BlockSpec(n.shape, lambda i: (0, 0)) for n in narrow],
        out_specs=pl.BlockSpec(out, (lambda i: (0, 0, i)) if turned else (lambda i: (0, i, 0))),
    )


def norm_kernel(places, queries, states, out_grad, *refs):
    blocks, local_back, norm_out = refs[:-2], refs[-2], refs[-1]
    spots = places[...]
    rows = blocks[0].shape[0]
    picks = [one_hot(pick(spots, 0, n, rows) | pick(spots, 1, n, rows)) for n in range(len(blocks))]
    if rows % 16:
        moe = dot_tn(picks[0], blocks[0][...])
        for chosen, block in zip(picks[1:], blocks[1:]):
            moe = moe + dot_tn(chosen, block[...])
    else:
        moe = dot_tn(jnp.concatenate(picks), jnp.concatenate([block[...] for block in blocks]))
    hidden_grads = out_grad[...].astype(F32) + moe
    for h in range(queries.shape[1] // HEAD_DIM):
        cols = head_cols(h)
        query, state = queries[:, cols], states[cols]
        mixed = dot(query, state)
        scale = lax.rsqrt(jnp.mean(mixed * mixed, axis=-1, keepdims=True) + EPSILON)
        normed = mixed * scale
        hidden_grad = hidden_grads[:, cols]
        norm_grad = scale * (hidden_grad - normed * jnp.mean(hidden_grad * normed, axis=-1, keepdims=True))
        norm_grad = norm_grad.astype(BF16)
        norm_out[:, cols] = norm_grad
        local_back[cols] = dot_tn(query, norm_grad).astype(BF16)


def query_kernel(norm_grad, states, query_grad):
    for h in range(norm_grad.shape[1] // HEAD_DIM):
        cols = head_cols(h)
        query_grad[:, cols] = dot_nt(norm_grad[:, cols], states[cols]).astype(BF16)


def key_kernel(keys, values, back, key_grad, value_grad):
    for h in range(keys.shape[1] // HEAD_DIM):
        cols = head_cols(h)
        state = back[cols]
        key_grad[:, cols] = dot_nt(values[:, cols], state).astype(BF16)
        value_grad[:, cols] = dot(keys[:, cols], state).astype(BF16)


def body(queries, keys, values, out_grad, expert_ids, combine_gates, gate_weight, up_weight, down_weight):
    tok_rows, width = queries.shape
    times, groups = lax.axis_size("tm"), lax.axis_size("eg")
    experts = times * groups
    devices = experts * SLICES
    per_span = groups * SLICES
    capacity = SLICES * max(1, 3 * tok_rows // (experts * SLICES))
    halves = 1
    first_g, first_h, first_back = (2, 1), (2, 2), (2, 2)
    others = range(1, groups)

    def to_owners(terms):
        return exchange(terms, ALL)

    def span_sums(got, backward):
        rows = got.shape[0] // devices
        got = got.reshape(times, per_span, rows, HEAD_DIM).astype(F32)
        spans = jnp.sum(got, axis=1)
        order = range(times - 1, -1, -1) if backward else range(times)
        total, sums = None, [None] * times
        for c in order:
            total = spans[c] if total is None else total + spans[c]
            sums[c] = total
        sums = jnp.stack(sums).astype(BF16)
        send = jnp.broadcast_to(sums[:, None], (times, per_span, rows, HEAD_DIM))
        return send.reshape(devices * rows, HEAD_DIM)

    me = lax.axis_index("tm") * groups + lax.axis_index("eg")
    ids = expert_ids.T
    spots = slot_places(expert_ids, capacity, experts).reshape(tok_rows, 2).T
    kept = spots < experts * capacity
    position = jnp.where(kept, spots - ids * capacity, -1)
    info = jnp.concatenate([ids.astype(F32), position.astype(F32), combine_gates.T, jnp.zeros((2, tok_rows), F32)])

    def localize(info):
        ids, position = info[:2].astype(jnp.int32), info[2:4].astype(jnp.int32)
        places = jnp.where(position < 0, -1, (ids ^ me) * capacity + position)
        return jnp.concatenate([places.astype(F32), info[4:6], jnp.zeros((4, tok_rows), F32)])

    def from_group(value, f):
        return lax.ppermute(value, "eg", [(i, i ^ f) for i in range(groups)])

    own_info = localize(info)
    places = own_info[:2].astype(jnp.int32)
    near_infos = [own_info] + [localize(swap(info, s)) for s in range(1, SLICES)]
    far_infos = [None] + [localize(from_group(info, f)) for f in others]

    def trade_times(blocks):
        moved = list(blocks)
        for q in range(1, times):
            moved[q] = lax.ppermute(blocks[q], "tm", [(i, i ^ q) for i in range(times)])
        return moved

    def dispatch(tokens, firsts, scaled):
        far_tokens = [from_group(tokens, f) for f in others]
        square = spread(tokens, firsts[0])
        far = []
        for f, other in zip(others, far_tokens):
            blocks = slots([far_infos[f]], [other], capacity, times, groups, scaled)
            blocks = trade_times(blocks)
            far.append(spread(join(blocks), firsts[1]))
        near = slots(near_infos, [square[s] for s in range(SLICES)], capacity, times, groups, scaled)
        return trade_times(near), far

    terms = call(outer_kernel, like((width, HEAD_DIM)), keys, values)
    got_terms = to_owners(terms)
    near_g, far_g = dispatch(out_grad, first_g, True)
    states = exchange(span_sums(got_terms, False), ALL)
    hidden = call(hidden_kernel, like((tok_rows, width)), queries, states)
    near_h, far_h = dispatch(hidden, first_h, False)

    gate_w, up_w, down_w = gate_weight[0], up_weight[0], down_weight[0]
    xs, ys, acts, ggs, ugs, parts = [], [], [], [], [], {}

    def expert(x, y, keys_, regroup=False):
        grads = act_grads(y, down_w)
        act, gg, ug, part = expert_rows(x, grads, gate_w, up_w, halves, len(keys_), regroup)
        for key, pair in zip(keys_, part):
            parts[key] = pair
        xs.extend(x)
        ys.extend(y)
        acts.append(act)
        ggs.append(gg)
        ugs.append(ug)

    expert(near_h, near_g, [(0, s) for s in range(SLICES)], True)
    for f in others:
        x, y = far_h[f - 1], far_g[f - 1]
        for group in ((0, 1, 2), (3,)):
            expert([x[s] for s in group], [y[s] for s in group], [(f, s) for s in group])

    returns = []
    for j in range(halves):
        blocks = [None] * experts
        for p in range(groups):
            first = first_back[p > 0]
            other = 3 - first
            far_in = swap(parts[p, 3][j], other)
            own_in = swap(parts[p, other][j], other)
            mid = add_up([parts[p, first][j], far_in])
            mid_in = swap(mid, first)
            total = add_up([parts[p, 0][j], own_in, mid_in], times)
            for q in range(times):
                blocks[q * groups + p] = total[q]
        returns.append(trade(blocks))

    gate_wgrad = weight_grad(xs, ggs, False)
    up_wgrad = weight_grad(xs, ugs, False)
    down_wgrad = weight_grad(ys, acts, True)

    local_back, norm_grad = call(
        norm_kernel, [like((width, HEAD_DIM)), like((tok_rows, width))],
        places, queries, states, out_grad, *returns[0],
    )
    query_grad = call(query_kernel, like((tok_rows, width)), norm_grad, states)
    sums = span_sums(to_owners(local_back), True)
    back = exchange(sums, ALL)
    key_grad, value_grad = call(key_kernel, [like(keys.shape)] * 2, keys, values, back)
    return query_grad, key_grad, value_grad, gate_wgrad, up_wgrad, down_wgrad


def solution(mesh):
    times, members = mesh.devices.shape
    fine = Mesh(mesh.devices.reshape(times, members // SLICES, SLICES), ALL)
    two, three = P(ALL, None), P(ALL, None, None)
    return jax.shard_map(
        body,
        mesh=fine,
        in_specs=(two,) * 6 + (three,) * 3,
        out_specs=(two,) * 3 + (three,) * 3,
        check_vma=False,
    )
```

profile of v0, /device:TPU:0, one launch (start us, length us, event | category | flops | bytes accessed | tf_op | source)
XLA Modules:
  0.0 380.7 jit_solution(10898061796384646660)
XLA Ops:
  3.0 7.3 %all-to-all-start = ((bf16[32,64,128]{2,1,0:T(8,128)(2,1)}), bf16[32,64,128]{2,1,0:T(8,128)(2,1)S(1)}, u32[]{:S(2)}, u32[]{:S(2)}) async-start(bf16[32,64,128]{2,1,0:T(8,128)(2,1)} %bitcast.46), calls=%async_computation | async-start | bytes 1048576 | tf_op jit(solution)/shard_map/all_to_all | solution.py:47
  12.1 14.5 %all-to-all-done = bf16[32,64,128]{2,1,0:T(8,128)(2,1)S(1)} async-done(((bf16[32,64,128]{2,1,0:T(8,128)(2,1)}), bf16[32,64,128]{2,1,0:T(8,128)(2,1)S(1)}, u32[]{:S(2)}, u32[]{:S(2)}) %all-to-all-start) | async-done | bytes 524320 | tf_op jit(solution)/shard_map/all_to_all | solution.py:47
  39.1 6.3 %collective-permute-done.18 = f32[8,128]{1,0:T(8,128)S(1)} collective-permute-done((f32[8,128]{1,0:T(8,128)S(1)}, f32[8,128]{1,0:T(8,128)S(1)}, u32[]{:S(2)}, u32[]{:S(2)}) %collective-permute-start.18) | collective-permute-done | bytes 4128 | tf_op jit(solution)/shard_map/ppermute | solution.py:321
  54.5 18.0 %collective-permute-done.25.refs_1_ = bf16[128,2048]{1,0:T(8,128)(2,1)S(1)} collective-permute-done((bf16[128,2048]{1,0:T(8,128)(2,1)S(1)}, bf16[128,2048]{1,0:T(8,128)(2,1)S(1)}, u32[]{:S(2)}, u32[]{:S(2)}) %collective-permute-start.25) | collective-permute-done | bytes 524320 | tf_op jit(solution)/shard_map/ppermute | solution.py:321
  79.4 11.8 %collective-permute-done.4.refs_6_ = bf16[128,2048]{1,0:T(8,128)(2,1)} collective-permute-done((bf16[128,2048]{1,0:T(8,128)(2,1)}, bf16[128,2048]{1,0:T(8,128)(2,1)}, u32[]{:S(2)}, u32[]{:S(2)}) %collective-permute-start.4) | collective-permute-done | bytes 524320 | tf_op jit(solution)/shard_map/ppermute | solution.py:43
  103.4 4.5 %shard_map.139 = (bf16[192,2048]{1,0:T(8,128)(2,1)}, bf16[192,2048]{1,0:T(8,128)(2,1)}, bf16[192,2048]{1,0:T(8,128)(2,1)}, bf16[192,2048]{1,0:T(8,128)(2,1)}) custom-call(f32[8,128]{1,0:T(8,128)} %get-tuple-element.105.refs_0_, f32[8,128]{1,0:T(8,128)} %get-tuple-element.109.refs_1_, f32[8,128]{1,0:T(8,128)} %get-tuple-element.110.refs_2_, ...), custom_call_target="tpu_custom_call" | custom-call | tf_op jit(solution)/shard_map/pallas_call | solution.py:31
  110.9 4.5 %collective-permute-done.22.refs_3_ = bf16[48,2048]{1,0:T(8,128)(2,1)S(1)} collective-permute-done((bf16[48,2048]{1,0:T(8,128)(2,1)S(1)}, bf16[48,2048]{1,0:T(8,128)(2,1)S(1)}, u32[]{:S(2)}, u32[]{:S(2)}) %collective-permute-start.22) | collective-permute-done | bytes 196640 | tf_op jit(solution)/shard_map/ppermute | solution.py:331
  119.7 4.2 %shard_map.138 = (bf16[192,2048]{1,0:T(8,128)(2,1)}, bf16[192,2048]{1,0:T(8,128)(2,1)}, bf16[192,2048]{1,0:T(8,128)(2,1)}, bf16[192,2048]{1,0:T(8,128)(2,1)}) custom-call(f32[8,128]{1,0:T(8,128)} %get-tuple-element.105.refs_0_, f32[8,128]{1,0:T(8,128)} %get-tuple-element.109.refs_1_, f32[8,128]{1,0:T(8,128)} %get-tuple-element.110.refs_2_, ...), custom_call_target="tpu_custom_call" | custom-call | tf_op jit(solution)/shard_map/pallas_call | solution.py:31
  123.9 5.5 %collective-permute-done.29.refs_1_.refs_5_ = bf16[192,2048]{1,0:T(8,128)(2,1)S(1)} collective-permute-done((bf16[192,2048]{1,0:T(8,128)(2,1)}, bf16[192,2048]{1,0:T(8,128)(2,1)S(1)}, u32[]{:S(2)}, u32[]{:S(2)}) %collective-permute-start.29) | collective-permute-done | bytes 786464 | tf_op jit(solution)/shard_map/ppermute | solution.py:43
  134.4 14.8 %collective-permute-done.14.refs_3_ = bf16[192,2048]{1,0:T(8,128)(2,1)} collective-permute-done((bf16[192,2048]{1,0:T(8,128)(2,1)}, bf16[192,2048]{1,0:T(8,128)(2,1)}, u32[]{:S(2)}, u32[]{:S(2)}) %collective-permute-start.14) | collective-permute-done | bytes 786464 | tf_op jit(solution)/shard_map/ppermute | solution.py:331
  149.4 5.6 %shard_map.140.refs_4_ = f32[768,512]{1,0:T(8,128)} custom-call(bf16[192,2048]{1,0:T(8,128)(2,1)} %get-tuple-element.55.refs_0_, bf16[192,2048]{1,0:T(8,128)(2,1)} %copy-done.8, bf16[192,2048]{1,0:T(8,128)(2,1)} %copy-done.9, bf16[192,2048]{1,0:T(8,128)(2,1)} %collective-permute-done.14.refs_3_, bf16[512,2048]{1,0:T(8,128)(2,1)} %bitcast.34), custom_call_target="tpu_custom_call" | custom-call | tf_op jit(solution)/shard_map/pallas_call | solution.py:31
  155.0 12.2 %collective-permute-done.7.refs_2_ = bf16[192,2048]{1,0:T(8,128)(2,1)S(1)} collective-permute-done((bf16[192,2048]{1,0:T(8,128)(2,1)}, bf16[192,2048]{1,0:T(8,128)(2,1)S(1)}, u32[]{:S(2)}, u32[]{:S(2)}) %collective-permute-start.7) | collective-permute-done | bytes 786464 | tf_op jit(solution)/shard_map/ppermute | solution.py:331
  167.2 15.5 %collective-permute-done.8.refs_3_ = bf16[192,2048]{1,0:T(8,128)(2,1)S(1)} collective-permute-done((bf16[192,2048]{1,0:T(8,128)(2,1)}, bf16[192,2048]{1,0:T(8,128)(2,1)S(1)}, u32[]{:S(2)}, u32[]{:S(2)}) %collective-permute-start.8) | collective-permute-done | bytes 786464 | tf_op jit(solution)/shard_map/ppermute | solution.py:331
  183.6 12.2 %shard_map.141 = (bf16[768,512]{1,0:T(8,128)(2,1)}, bf16[768,512]{1,0:T(8,128)(2,1)}, bf16[768,512]{1,0:T(8,128)(2,1)}, bf16[192,2048]{1,0:T(8,128)(2,1)}, bf16[...) custom-call(bf16[192,2048]{1,0:T(8,128)(2,1)} %get-tuple-element.51.refs_0_, ...), custom_call_target="tpu_custom_call" | custom-call | tf_op jit(solution)/shard_map/pallas_call | solution.py:31
  196.0 3.5 shard_map.150.refs_1_
  201.3 5.9 %shard_map.151 = (bf16[192,512]{1,0:T(8,128)(2,1)}, bf16[192,512]{1,0:T(8,128)(2,1)}, bf16[192,512]{1,0:T(8,128)(2,1)}, bf16[192,2048]{1,0:T(8,128)(2,1)}) custom-call(bf16[192,2048]{1,0:T(8,128)(2,1)} %collective-permute-done.32.refs_0_.refs_7_, f32[192,512]{1,0:T(8,128)} %shard_map.150.refs_1_, bf16[2048,512]{1,0:T(8,128)(2,1)} %bitcast.38, ...), custom_call_target="tpu_custom_call" | custom-call | tf_op jit(solution)/shard_map/pallas_call | solution.py:31
  209.2 7.3 %collective-permute-done.16.refs_1_ = bf16[192,2048]{1,0:T(8,128)(2,1)} collective-permute-done((bf16[192,2048]{1,0:T(8,128)(2,1)}, bf16[192,2048]{1,0:T(8,128)(2,1)}, u32[]{:S(2)}, u32[]{:S(2)}) %collective-permute-start.16) | collective-permute-done | bytes 786464 | tf_op jit(solution)/shard_map/ppermute | solution.py:43
  219.9 4.7 %shard_map.148.refs_3_ = f32[576,512]{1,0:T(8,128)} custom-call(bf16[192,2048]{1,0:T(8,128)(2,1)} %shard_map.147.refs_0_.refs_4_, bf16[192,2048]{1,0:T(8,128)(2,1)} %copy-done.7, bf16[192,2048]{1,0:T(8,128)(2,1)} %copy-done.10, bf16[512,2048]{1,0:T(8,128)(2,1)} %bitcast.36), custom_call_target="tpu_custom_call" | custom-call | tf_op jit(solution)/shard_map/pallas_call | solution.py:31
  224.6 8.6 %collective-permute-done.23.refs_1_.refs_5_ = bf16[192,2048]{1,0:T(8,128)(2,1)S(1)} collective-permute-done((bf16[192,2048]{1,0:T(8,128)(2,1)S(1)}, bf16[192,2048]{1,0:T(8,128)(2,1)S(1)}, u32[]{:S(2)}, u32[]{:S(2)}) %collective-permute-start.23) | collective-permute-done | bytes 786464 | tf_op jit(solution)/shard_map/ppermute | solution.py:43
  234.2 9.9 %shard_map.149 = (bf16[576,512]{1,0:T(8,128)(2,1)}, bf16[576,512]{1,0:T(8,128)(2,1)}, bf16[576,512]{1,0:T(8,128)(2,1)}, bf16[192,2048]{1,0:T(8,128)(2,1)}, bf16[...) custom-call(bf16[192,2048]{1,0:T(8,128)(2,1)} %shard_map.145.refs_0_.refs_4_, bf16[192,2048]{1,0:T(8,128)(2,1)} %copy-done.6, ...), custom_call_target="tpu_custom_call" | custom-call | tf_op jit(solution)/shard_map/pallas_call | solution.py:31
  244.2 6.0 %collective-permute-done.34.refs_1_ = bf16[192,2048]{1,0:T(8,128)(2,1)} collective-permute-done((bf16[192,2048]{1,0:T(8,128)(2,1)}, bf16[192,2048]{1,0:T(8,128)(2,1)}, u32[]{:S(2)}, u32[]{:S(2)}) %collective-permute-start.34) | collective-permute-done | bytes 786464 | tf_op jit(solution)/shard_map/ppermute | solution.py:43
  252.7 14.3 %collective-permute-done.15.refs_1_ = bf16[192,2048]{1,0:T(8,128)(2,1)S(1)} collective-permute-done((bf16[192,2048]{1,0:T(8,128)(2,1)}, bf16[192,2048]{1,0:T(8,128)(2,1)S(1)}, u32[]{:S(2)}, u32[]{:S(2)}) %collective-permute-start.15) | collective-permute-done | bytes 786464 | tf_op jit(solution)/shard_map/ppermute | solution.py:43
  272.3 11.1 %collective-permute-done.31.refs_1_ = bf16[192,2048]{1,0:T(8,128)(2,1)S(1)} collective-permute-done((bf16[192,2048]{1,0:T(8,128)(2,1)}, bf16[192,2048]{1,0:T(8,128)(2,1)S(1)}, u32[]{:S(2)}, u32[]{:S(2)}) %collective-permute-start.31) | collective-permute-done | bytes 786464 | tf_op jit(solution)/shard_map/ppermute | solution.py:43
  293.3 17.8 %collective-permute-done.36.refs_1_ = bf16[48,2048]{1,0:T(8,128)(2,1)S(1)} collective-permute-done((bf16[48,2048]{1,0:T(8,128)(2,1)}, bf16[48,2048]{1,0:T(8,128)(2,1)S(1)}, u32[]{:S(2)}, u32[]{:S(2)}) %collective-permute-start.36) | collective-permute-done | bytes 196640 | tf_op jit(solution)/shard_map/ppermute | solution.py:54
  311.0 4.0 %collective-permute-done.38.refs_3_ = bf16[48,2048]{1,0:T(8,128)(2,1)S(1)} collective-permute-done((bf16[48,2048]{1,0:T(8,128)(2,1)}, bf16[48,2048]{1,0:T(8,128)(2,1)S(1)}, u32[]{:S(2)}, u32[]{:S(2)}) %collective-permute-start.38) | collective-permute-done | bytes 196640 | tf_op jit(solution)/shard_map/ppermute | solution.py:54
  315.1 4.9 %collective-permute-done.40.refs_5_ = bf16[48,2048]{1,0:T(8,128)(2,1)S(1)} collective-permute-done((bf16[48,2048]{1,0:T(8,128)(2,1)}, bf16[48,2048]{1,0:T(8,128)(2,1)S(1)}, u32[]{:S(2)}, u32[]{:S(2)}) %collective-permute-start.40) | collective-permute-done | bytes 196640 | tf_op jit(solution)/shard_map/ppermute | solution.py:54
  320.0 4.0 %collective-permute-done.42.refs_7_ = bf16[48,2048]{1,0:T(8,128)(2,1)S(1)} collective-permute-done((bf16[48,2048]{1,0:T(8,128)(2,1)}, bf16[48,2048]{1,0:T(8,128)(2,1)S(1)}, u32[]{:S(2)}, u32[]{:S(2)}) %collective-permute-start.42) | collective-permute-done | bytes 196640 | tf_op jit(solution)/shard_map/ppermute | solution.py:54
  324.7 4.0 %shard_map.154 = (bf16[2048,128]{1,0:T(8,128)(2,1)}, bf16[128,2048]{1,0:T(8,128)(2,1)}) custom-call(s32[2,128]{1,0:T(2,128)} %get-tuple-element.96.places, bf16[128,2048]{1,0:T(8,128)(2,1)} %queries.3, bf16[2048,128]{1,0:T(8,128)(2,1)} %bitcast.44, bf16[128,2048]{1,0:T(8,128)(2,1)} %out_grad.1, bf16[48,2048]{1,0:T(8,128)(2,1)} %get-tuple-element.63.refs_0_, ...), custom_call_target="tpu_custom_call" | custom-call | tf_op jit(solution)/shard_map/pallas_call | solution.py:31
  328.7 18.8 %all_to_all.40 = bf16[32,64,128]{2,1,0:T(8,128)(2,1)S(1)} all-to-all(bf16[32,64,128]{2,1,0:T(8,128)(2,1)} %bitcast.48), channel_id=1, replica_groups=mesh['tm'=4,'eg'=2,'sl'=4] {'tm','eg','sl'}, dimensions={0} | all-to-all | bytes 1048576 | tf_op jit(solution)/shard_map/all_to_all | solution.py:47
  351.4 7.7 %shard_map.157 = f32[1,2048,512]{2,1,0:T(8,128)} custom-call(bf16[192,2048]{1,0:T(8,128)(2,1)} %get-tuple-element.51.refs_0_, bf16[192,2048]{1,0:T(8,128)(2,1)} %copy-done.3, bf16[192,2048]{1,0:T(8,128)(2,1)} %copy-done.4, bf16[192,2048]{1,0:T(8,128)(2,1)} %copy-done.5, bf16[192,2048]{1,0:T(8,128)(2,1)} %shard_map.145.refs_0_.refs_4_, ...), custom_call_target="tpu_custom_call" | custom-call | tf_op jit(solution)/shard_map/pallas_call | solution.py:31
  359.1 7.7 %shard_map.158 = f32[1,2048,512]{2,1,0:T(8,128)} custom-call(bf16[192,2048]{1,0:T(8,128)(2,1)} %get-tuple-element.51.refs_0_, bf16[192,2048]{1,0:T(8,128)(2,1)} %copy-done.3, bf16[192,2048]{1,0:T(8,128)(2,1)} %copy-done.4, bf16[192,2048]{1,0:T(8,128)(2,1)} %copy-done.5, bf16[192,2048]{1,0:T(8,128)(2,1)} %shard_map.145.refs_0_.refs_4_, ...), custom_call_target="tpu_custom_call" | custom-call | tf_op jit(solution)/shard_map/pallas_call | solution.py:31
  366.7 7.8 %shard_map.159 = f32[1,512,2048]{2,1,0:T(8,128)} custom-call(bf16[192,2048]{1,0:T(8,128)(2,1)} %get-tuple-element.55.refs_0_, bf16[192,2048]{1,0:T(8,128)(2,1)} %copy-done.8, bf16[192,2048]{1,0:T(8,128)(2,1)} %copy-done.9, bf16[192,2048]{1,0:T(8,128)(2,1)} %collective-permute-done.14.refs_3_, bf16[192,2048]{1,0:T(8,128)(2,1)} %shard_map.147.refs_0_.refs_4_, ...), custom_call_target="tpu_custom_call" | custom-call | tf_op jit(solution)/shard_map/pallas_call | solution.py:31
  (196 shorter events, 94.9 us)
Async XLA Ops:
  3.0 23.6 %all-to-all-start = ((bf16[32,64,128]{2,1,0:T(8,128)(2,1)}), bf16[32,64,128]{2,1,0:T(8,128)(2,1)S(1)}, u32[]{:S(2)}, u32[]{:S(2)}) async-start(bf16[32,64,128]{2,1,0:T(8,128)(2,1)} %bitcast.46), calls=%async_computation | async-start | bytes 1048576 | tf_op jit(solution)/shard_map/all_to_all | solution.py:47
  37.6 39.7 %collective-permute-start.9 = (bf16[128,2048]{1,0:T(8,128)(2,1)S(1)}, bf16[128,2048]{1,0:T(8,128)(2,1)S(1)}, u32[]{:S(2)}, u32[]{:S(2)}) collective-permute-start(bf16[128,2048]{1,0:T(8,128)(2,1)S(1)} %copy-done.12), channel_id=1, source_target_pairs={{0,1},{1,0},{2,3},{3,2},{4,5},{5,4},{6,7},{7,6},{8,9},{9,8},{10,11... | collective-permute-start | bytes 1572872 | tf_op jit(solution)/shard_map/ppermute | solution.py:43
  45.4 30.4 %collective-permute-start.10 = (bf16[128,2048]{1,0:T(8,128)(2,1)S(1)}, bf16[128,2048]{1,0:T(8,128)(2,1)S(1)}, u32[]{:S(2)}, u32[]{:S(2)}) collective-permute-start(bf16[128,2048]{1,0:T(8,128)(2,1)S(1)} %copy-done.12), channel_id=1, source_target_pairs={{0,2},{1,3},{2,0},{3,1},{4,6},{5,7},{6,4},{7,5},{8,10},{9,11},{10,... | collective-permute-start | bytes 1572872 | tf_op jit(solution)/shard_map/ppermute | solution.py:43
  45.4 27.1 %collective-permute-start.25 = (bf16[128,2048]{1,0:T(8,128)(2,1)S(1)}, bf16[128,2048]{1,0:T(8,128)(2,1)S(1)}, u32[]{:S(2)}, u32[]{:S(2)}) collective-permute-start(bf16[128,2048]{1,0:T(8,128)(2,1)S(1)} %copy-done.12), channel_id=1, source_target_pairs={{0,4},{4,0},{1,5},{5,1},{2,6},{6,2},{3,7},{7,3},{8,12},{12,8},{9,1... | collective-permute-start | bytes 1572872 | tf_op jit(solution)/shard_map/ppermute | solution.py:321
  50.6 40.6 %collective-permute-start.4 = (bf16[128,2048]{1,0:T(8,128)(2,1)}, bf16[128,2048]{1,0:T(8,128)(2,1)}, u32[]{:S(2)}, u32[]{:S(2)}) collective-permute-start(bf16[128,2048]{1,0:T(8,128)(2,1)} %shard_map.137.refs_4_), channel_id=1, source_target_pairs={{0,2},{1,3},{2,0},{3,1},{4,6},{5,7},{6,4},{7,5},{8,10},{9,11},{10,... | collective-permute-start | bytes 1572872 | tf_op jit(solution)/shard_map/ppermute | solution.py:43
  50.8 42.4 %collective-permute-start.19 = (bf16[128,2048]{1,0:T(8,128)(2,1)}, bf16[128,2048]{1,0:T(8,128)(2,1)S(1)}, u32[]{:S(2)}, u32[]{:S(2)}) collective-permute-start(bf16[128,2048]{1,0:T(8,128)(2,1)} %shard_map.137.refs_4_), channel_id=1, source_target_pairs={{0,4},{4,0},{1,5},{5,1},{2,6},{6,2},{3,7},{7,3},{8,12},{12,8},{9,1... | collective-permute-start | bytes 1572872 | tf_op jit(solution)/shard_map/ppermute | solution.py:321
  75.7 25.8 %collective-permute-start.11 = (bf16[128,2048]{1,0:T(8,128)(2,1)S(1)}, bf16[128,2048]{1,0:T(8,128)(2,1)}, u32[]{:S(2)}, u32[]{:S(2)}) collective-permute-start(bf16[128,2048]{1,0:T(8,128)(2,1)S(1)} %collective-permute-done.10.refs_6_), channel_id=1, source_target_pairs={{0,1},{1,0},{2,3},{3,2},{4,5},{5,4},{6,7},{7,6},{8,9},{9,8},{10,11... | collective-permute-start | bytes 1572872 | tf_op jit(solution)/shard_map/ppermute | solution.py:43
  77.3 30.6 %collective-permute-start.3 = (bf16[128,2048]{1,0:T(8,128)(2,1)}, bf16[128,2048]{1,0:T(8,128)(2,1)S(1)}, u32[]{:S(2)}, u32[]{:S(2)}) collective-permute-start(bf16[128,2048]{1,0:T(8,128)(2,1)} %shard_map.137.refs_4_), channel_id=1, source_target_pairs={{0,1},{1,0},{2,3},{3,2},{4,5},{5,4},{6,7},{7,6},{8,9},{9,8},{10,11... | collective-permute-start | bytes 1572872 | tf_op jit(solution)/shard_map/ppermute | solution.py:43
  93.2 26.5 %collective-permute-start.5 = (bf16[128,2048]{1,0:T(8,128)(2,1)}, bf16[128,2048]{1,0:T(8,128)(2,1)}, u32[]{:S(2)}, u32[]{:S(2)}) collective-permute-start(bf16[128,2048]{1,0:T(8,128)(2,1)} %collective-permute-done.4.refs_6_), channel_id=1, source_target_pairs={{0,1},{1,0},{2,3},{3,2},{4,5},{5,4},{6,7},{7,6},{8,9},{9,8},{10,11... | collective-permute-start | bytes 1572872 | tf_op jit(solution)/shard_map/ppermute | solution.py:43
  101.5 27.9 %collective-permute-start.29 = (bf16[192,2048]{1,0:T(8,128)(2,1)}, bf16[192,2048]{1,0:T(8,128)(2,1)S(1)}, u32[]{:S(2)}, u32[]{:S(2)}) collective-permute-start(bf16[192,2048]{1,0:T(8,128)(2,1)} %shard_map.147.refs_0_.refs_4_), channel_id=1, source_target_pairs={{0,1},{1,0},{2,3},{3,2},{4,5},{5,4},{6,7},{7,6},{8,9},{9,8},{10,11... | collective-permute-start | bytes 2359304 | tf_op jit(solution)/shard_map/ppermute | solution.py:43
  108.7 21.6 %collective-permute-start.12 = (bf16[192,2048]{1,0:T(8,128)(2,1)}, bf16[192,2048]{1,0:T(8,128)(2,1)S(1)}, u32[]{:S(2)}, u32[]{:S(2)}) collective-permute-start(bf16[192,2048]{1,0:T(8,128)(2,1)} %get-tuple-element.56), channel_id=1, source_target_pairs={{0,8},{8,0},{16,24},{24,16},{1,9},{9,1},{17,25},{25,17},{2,10},{10... | collective-permute-start | bytes 2359304 | tf_op jit(solution)/shard_map/ppermute | solution.py:331
  110.1 23.4 %collective-permute-start.13 = (bf16[192,2048]{1,0:T(8,128)(2,1)}, bf16[192,2048]{1,0:T(8,128)(2,1)S(1)}, u32[]{:S(2)}, u32[]{:S(2)}) collective-permute-start(bf16[192,2048]{1,0:T(8,128)(2,1)} %get-tuple-element.57), channel_id=1, source_target_pairs={{0,16},{8,24},{16,0},{24,8},{1,17},{9,25},{17,1},{25,9},{2,18},{10... | collective-permute-start | bytes 2359304 | tf_op jit(solution)/shard_map/ppermute | solution.py:331
  115.4 33.8 %collective-permute-start.14 = (bf16[192,2048]{1,0:T(8,128)(2,1)}, bf16[192,2048]{1,0:T(8,128)(2,1)}, u32[]{:S(2)}, u32[]{:S(2)}) collective-permute-start(bf16[192,2048]{1,0:T(8,128)(2,1)} %get-tuple-element.58), channel_id=1, source_target_pairs={{0,24},{8,16},{16,8},{24,0},{1,25},{9,17},{17,9},{25,1},{2,26},{10... | collective-permute-start | bytes 2359304 | tf_op jit(solution)/shard_map/ppermute | solution.py:331
  119.7 29.4 %collective-permute-start.24 = (bf16[192,2048]{1,0:T(8,128)(2,1)}, bf16[192,2048]{1,0:T(8,128)(2,1)S(1)}, u32[]{:S(2)}, u32[]{:S(2)}) collective-permute-start(bf16[192,2048]{1,0:T(8,128)(2,1)} %shard_map.145.refs_0_.refs_4_), channel_id=1, source_target_pairs={{0,2},{1,3},{2,0},{3,1},{4,6},{5,7},{6,4},{7,5},{8,10},{9,11},{10,... | collective-permute-start | bytes 2359304 | tf_op jit(solution)/shard_map/ppermute | solution.py:43
  130.3 24.7 %collective-permute-start.6 = (bf16[192,2048]{1,0:T(8,128)(2,1)}, bf16[192,2048]{1,0:T(8,128)(2,1)S(1)}, u32[]{:S(2)}, u32[]{:S(2)}) collective-permute-start(bf16[192,2048]{1,0:T(8,128)(2,1)} %get-tuple-element.52), channel_id=1, source_target_pairs={{0,8},{8,0},{16,24},{24,16},{1,9},{9,1},{17,25},{25,17},{2,10},{10... | collective-permute-start | bytes 2359304 | tf_op jit(solution)/shard_map/ppermute | solution.py:331
  131.2 36.0 %collective-permute-start.7 = (bf16[192,2048]{1,0:T(8,128)(2,1)}, bf16[192,2048]{1,0:T(8,128)(2,1)S(1)}, u32[]{:S(2)}, u32[]{:S(2)}) collective-permute-start(bf16[192,2048]{1,0:T(8,128)(2,1)} %get-tuple-element.53), channel_id=1, source_target_pairs={{0,16},{8,24},{16,0},{24,8},{1,17},{9,25},{17,1},{25,9},{2,18},{10... | collective-permute-start | bytes 2359304 | tf_op jit(solution)/shard_map/ppermute | solution.py:331
  134.4 48.3 %collective-permute-start.8 = (bf16[192,2048]{1,0:T(8,128)(2,1)}, bf16[192,2048]{1,0:T(8,128)(2,1)S(1)}, u32[]{:S(2)}, u32[]{:S(2)}) collective-permute-start(bf16[192,2048]{1,0:T(8,128)(2,1)} %get-tuple-element.54), channel_id=1, source_target_pairs={{0,24},{8,16},{16,8},{24,0},{1,25},{9,17},{17,9},{25,1},{2,26},{10... | collective-permute-start | bytes 2359304 | tf_op jit(solution)/shard_map/ppermute | solution.py:331
  149.2 46.8 %collective-permute-start.33 = (bf16[192,2048]{1,0:T(8,128)(2,1)}, bf16[192,2048]{1,0:T(8,128)(2,1)}, u32[]{:S(2)}, u32[]{:S(2)}) collective-permute-start(bf16[192,2048]{1,0:T(8,128)(2,1)} %copy-done.7), channel_id=1, source_target_pairs={{0,2},{1,3},{2,0},{3,1},{4,6},{5,7},{6,4},{7,5},{8,10},{9,11},{10,... | collective-permute-start | bytes 2359304 | tf_op jit(solution)/shard_map/ppermute | solution.py:43
  149.2 52.1 %collective-permute-start.32 = (bf16[192,2048]{1,0:T(8,128)(2,1)S(1)}, bf16[192,2048]{1,0:T(8,128)(2,1)}, u32[]{:S(2)}, u32[]{:S(2)}) collective-permute-start(bf16[192,2048]{1,0:T(8,128)(2,1)S(1)} %collective-permute-done.24.refs_2_.refs_6_), channel_id=1, source_target_pairs={{0,1},{1,0},{2,3},{3,2},{4,5},{5,4},{6,7},{7,6},{8,9},{9,8},{10,11... | collective-permute-start | bytes 2359304 | tf_op jit(solution)/shard_map/ppermute | solution.py:43
  196.0 23.0 %collective-permute-start.30 = (bf16[192,2048]{1,0:T(8,128)(2,1)}, bf16[192,2048]{1,0:T(8,128)(2,1)S(1)}, u32[]{:S(2)}, u32[]{:S(2)}) collective-permute-start(bf16[192,2048]{1,0:T(8,128)(2,1)} %shard_map.147.refs_0_.refs_4_), channel_id=1, source_target_pairs={{0,2},{1,3},{2,0},{3,1},{4,6},{5,7},{6,4},{7,5},{8,10},{9,11},{10,... | collective-permute-start | bytes 2359304 | tf_op jit(solution)/shard_map/ppermute | solution.py:43
  199.5 33.8 %collective-permute-start.23 = (bf16[192,2048]{1,0:T(8,128)(2,1)S(1)}, bf16[192,2048]{1,0:T(8,128)(2,1)S(1)}, u32[]{:S(2)}, u32[]{:S(2)}) collective-permute-start(bf16[192,2048]{1,0:T(8,128)(2,1)S(1)} %copy-done), channel_id=1, source_target_pairs={{0,1},{1,0},{2,3},{3,2},{4,5},{5,4},{6,7},{7,6},{8,9},{9,8},{10,11... | collective-permute-start | bytes 2359304 | tf_op jit(solution)/shard_map/ppermute | solution.py:43
  207.2 43.0 %collective-permute-start.34 = (bf16[192,2048]{1,0:T(8,128)(2,1)}, bf16[192,2048]{1,0:T(8,128)(2,1)}, u32[]{:S(2)}, u32[]{:S(2)}) collective-permute-start(bf16[192,2048]{1,0:T(8,128)(2,1)} %get-tuple-element.75), channel_id=1, source_target_pairs={{0,1},{1,0},{2,3},{3,2},{4,5},{5,4},{6,7},{7,6},{8,9},{9,8},{10,11... | collective-permute-start | bytes 2359304 | tf_op jit(solution)/shard_map/ppermute | solution.py:43
  207.4 59.6 %collective-permute-start.15 = (bf16[192,2048]{1,0:T(8,128)(2,1)}, bf16[192,2048]{1,0:T(8,128)(2,1)S(1)}, u32[]{:S(2)}, u32[]{:S(2)}) collective-permute-start(bf16[192,2048]{1,0:T(8,128)(2,1)} %get-tuple-element.60), channel_id=1, source_target_pairs={{0,1},{1,0},{2,3},{3,2},{4,5},{5,4},{6,7},{7,6},{8,9},{9,8},{10,11... | collective-permute-start | bytes 2359304 | tf_op jit(solution)/shard_map/ppermute | solution.py:43
  219.0 48.0 %collective-permute-start.17 = (bf16[192,2048]{1,0:T(8,128)(2,1)}, bf16[192,2048]{1,0:T(8,128)(2,1)}, u32[]{:S(2)}, u32[]{:S(2)}) collective-permute-start(bf16[192,2048]{1,0:T(8,128)(2,1)} %shard_map.142), channel_id=1, source_target_pairs={{0,2},{1,3},{2,0},{3,1},{4,6},{5,7},{6,4},{7,5},{8,10},{9,11},{10,... | collective-permute-start | bytes 2359304 | tf_op jit(solution)/shard_map/ppermute | solution.py:43
  244.0 39.3 %collective-permute-start.31 = (bf16[192,2048]{1,0:T(8,128)(2,1)}, bf16[192,2048]{1,0:T(8,128)(2,1)S(1)}, u32[]{:S(2)}, u32[]{:S(2)}) collective-permute-start(bf16[192,2048]{1,0:T(8,128)(2,1)} %get-tuple-element.73), channel_id=1, source_target_pairs={{0,1},{1,0},{2,3},{3,2},{4,5},{5,4},{6,7},{7,6},{8,9},{9,8},{10,11... | collective-permute-start | bytes 2359304 | tf_op jit(solution)/shard_map/ppermute | solution.py:43
  252.7 30.7 %collective-permute-start.35 = (bf16[192,2048]{1,0:T(8,128)(2,1)}, bf16[192,2048]{1,0:T(8,128)(2,1)S(1)}, u32[]{:S(2)}, u32[]{:S(2)}) collective-permute-start(bf16[192,2048]{1,0:T(8,128)(2,1)} %shard_map.152), channel_id=1, source_target_pairs={{0,2},{1,3},{2,0},{3,1},{4,6},{5,7},{6,4},{7,5},{8,10},{9,11},{10,... | collective-permute-start | bytes 2359304 | tf_op jit(solution)/shard_map/ppermute | solution.py:43
  271.6 21.6 %collective-permute-start.41 = (bf16[48,2048]{1,0:T(8,128)(2,1)}, bf16[48,2048]{1,0:T(8,128)(2,1)S(1)}, u32[]{:S(2)}, u32[]{:S(2)}) collective-permute-start(bf16[48,2048]{1,0:T(8,128)(2,1)} %get-tuple-element.81), channel_id=1, source_target_pairs={{0,24},{4,28},{8,16},{12,20},{16,8},{20,12},{24,0},{28,4},{1,25},{... | collective-permute-start | bytes 589832 | tf_op jit(solution)/shard_map/ppermute | solution.py:54
  287.1 24.0 %collective-permute-start.36 = (bf16[48,2048]{1,0:T(8,128)(2,1)}, bf16[48,2048]{1,0:T(8,128)(2,1)S(1)}, u32[]{:S(2)}, u32[]{:S(2)}) collective-permute-start(bf16[48,2048]{1,0:T(8,128)(2,1)} %get-tuple-element.76), channel_id=1, source_target_pairs={{0,4},{4,0},{8,12},{12,8},{16,20},{20,16},{24,28},{28,24},{1,5},{5... | collective-permute-start | bytes 589832 | tf_op jit(solution)/shard_map/ppermute | solution.py:54
  287.2 27.8 %collective-permute-start.38 = (bf16[48,2048]{1,0:T(8,128)(2,1)}, bf16[48,2048]{1,0:T(8,128)(2,1)S(1)}, u32[]{:S(2)}, u32[]{:S(2)}) collective-permute-start(bf16[48,2048]{1,0:T(8,128)(2,1)} %get-tuple-element.78), channel_id=1, source_target_pairs={{0,12},{4,8},{8,4},{12,0},{16,28},{20,24},{24,20},{28,16},{1,13},{... | collective-permute-start | bytes 589832 | tf_op jit(solution)/shard_map/ppermute | solution.py:54
  289.0 31.0 %collective-permute-start.40 = (bf16[48,2048]{1,0:T(8,128)(2,1)}, bf16[48,2048]{1,0:T(8,128)(2,1)S(1)}, u32[]{:S(2)}, u32[]{:S(2)}) collective-permute-start(bf16[48,2048]{1,0:T(8,128)(2,1)} %get-tuple-element.80), channel_id=1, source_target_pairs={{0,20},{4,16},{8,28},{12,24},{16,4},{20,0},{24,12},{28,8},{1,21},{... | collective-permute-start | bytes 589832 | tf_op jit(solution)/shard_map/ppermute | solution.py:54
  290.7 33.3 %collective-permute-start.42 = (bf16[48,2048]{1,0:T(8,128)(2,1)}, bf16[48,2048]{1,0:T(8,128)(2,1)S(1)}, u32[]{:S(2)}, u32[]{:S(2)}) collective-permute-start(bf16[48,2048]{1,0:T(8,128)(2,1)} %get-tuple-element.82), channel_id=1, source_target_pairs={{0,28},{4,24},{8,20},{12,16},{16,12},{20,8},{24,4},{28,0},{1,29},{... | collective-permute-start | bytes 589832 | tf_op jit(solution)/shard_map/ppermute | solution.py:54
  348.5 28.5 %all-to-all-start.3 = ((bf16[32,64,128]{2,1,0:T(8,128)(2,1)}), bf16[32,64,128]{2,1,0:T(8,128)(2,1)S(1)}, u32[]{:S(2)}, u32[]{:S(2)}) async-start(bf16[32,64,128]{2,1,0:T(8,128)(2,1)} %bitcast.14), calls=%async_computation.3 | async-start | bytes 1048576 | tf_op jit(solution)/shard_map/all_to_all | solution.py:47
  (51 other events, 560.3 us)
where the time goes:
time: 382 us; the launch traced here: 381 us
  waiting for transfers between devices  185 us (48%)
  Pallas kernels  107 us (28%)
  starting transfers between devices  52 us (14%)
  blocking collectives  18.8 us (5%)
  local copies, waits for them, and re-layouts  14.1 us (4%)
    pallas_call x24, Pallas kernels, call(): return pl.pallas_call(kernel, out_shape=out_shape, **options)(*args)  107 us
    ppermute x21, waiting for transfers between devices, swap(): return lax.ppermute(value, 'sl', [(i, i ^ bit) for i in range(SLICES)])  64.7 us
    ppermute x12, waiting for transfers between devices, trade_times(): moved[q] = lax.ppermute(blocks[q], 'tm', [(i, i ^ q) for i in range(times)])  49 us
    ppermute x7, waiting for transfers between devices, trade(): lax.ppermute(blocks[k], ('tm', 'eg'), [(i, i ^ k) for i in range(count)])  30.7 us
    ppermute x3, waiting for transfers between devices, from_group(): return lax.ppermute(value, 'eg', [(i, i ^ f) for i in range(groups)])  26.1 us
    all_to_all x1, blocking collectives, exchange(): return lax.all_to_all(value, axes, split_axis=0, concat_axis=0, tiled=True)  18.8 us
    ppermute x21, starting transfers between devices, swap(): return lax.ppermute(value, 'sl', [(i, i ^ bit) for i in range(SLICES)])  15.2 us
    all_to_all x3, waiting for transfers between devices, exchange(): return lax.all_to_all(value, axes, split_axis=0, concat_axis=0, tiled=True)  14.5 us
  transfers between devices with their start and end apart: 46, of which 21 were waited for; matrix products, arithmetic and copies ran while one was open for 1% of the time, Pallas kernels for 26%

commit v1 on v0

--- a/solution.py
+++ b/solution.py
@@ -239,18 +239,23 @@
     )
 
 
-def norm_kernel(places, queries, states, out_grad, *refs):
+def norm_kernel(halves, places, queries, states, out_grad, *refs):
     blocks, local_back, norm_out = refs[:-2], refs[-2], refs[-1]
     spots = places[...]
+    count = len(blocks) // halves
     rows = blocks[0].shape[0]
-    picks = [one_hot(pick(spots, 0, n, rows) | pick(spots, 1, n, rows)) for n in range(len(blocks))]
-    if rows % 16:
-        moe = dot_tn(picks[0], blocks[0][...])
-        for chosen, block in zip(picks[1:], blocks[1:]):
-            moe = moe + dot_tn(chosen, block[...])
-    else:
-        moe = dot_tn(jnp.concatenate(picks), jnp.concatenate([block[...] for block in blocks]))
-    hidden_grads = out_grad[...].astype(F32) + moe
+    picks = [one_hot(pick(spots, 0, n, rows) | pick(spots, 1, n, rows)) for n in range(count)]
+    moe = []
+    for j in range(halves):
+        mine = blocks[j * count : (j + 1) * count]
+        if rows % 16:
+            part = dot_tn(picks[0], mine[0][...])
+            for chosen, block in zip(picks[1:], mine[1:]):
+                part = part + dot_tn(chosen, block[...])
+        else:
+            part = dot_tn(jnp.concatenate(picks), jnp.concatenate([block[...] for block in mine]))
+        moe.append(part)
+    hidden_grads = out_grad[...].astype(F32) + jnp.concatenate(moe, axis=1)
     for h in range(queries.shape[1] // HEAD_DIM):
         cols = head_cols(h)
         query, state = queries[:, cols], states[cols]
@@ -285,8 +290,8 @@
     devices = experts * SLICES
     per_span = groups * SLICES
     capacity = SLICES * max(1, 3 * tok_rows // (experts * SLICES))
-    halves = 1
-    first_g, first_h, first_back = (2, 1), (2, 2), (2, 2)
+    halves = 2
+    first_g, first_h, first_back = (2, 1), (2, 2), ((1, 2), (2, 2))
     others = range(1, groups)
 
     def to_owners(terms):
@@ -373,7 +378,7 @@
     for j in range(halves):
         blocks = [None] * experts
         for p in range(groups):
-            first = first_back[p > 0]
+            first = first_back[j][p > 0]
             other = 3 - first
             far_in = swap(parts[p, 3][j], other)
             own_in = swap(parts[p, other][j], other)
@@ -389,8 +394,8 @@
     down_wgrad = weight_grad(ys, acts, True)
 
     local_back, norm_grad = call(
-        norm_kernel, [like((width, HEAD_DIM)), like((tok_rows, width))],
-        places, queries, states, out_grad, *returns[0],
+        functools.partial(norm_kernel, halves), [like((width, HEAD_DIM)), like((tok_rows, width))],
+        places, queries, states, out_grad, *sum(returns, []),
     )
     query_grad = call(query_kernel, like((tok_rows, width)), norm_grad, states)
     sums = span_sums(to_owners(local_back), True)

time: 382 us -> 355 us (0.929)
  waiting for transfers between devices: 185 us -> 146 us
  starting transfers between devices: 52 us -> 61.7 us
  Pallas kernels: 107 us -> 112 us
    ppermute x21 -> x27, waiting for transfers between devices: 64.7 us -> 44.7 us  [swap(): return lax.ppermute(value, 'sl', [(i, i ^ bit) for i in range(SLICES)])]
    all_to_all x3, waiting for transfers between devices: 14.5 us -> 1.17 us  [exchange(): return lax.all_to_all(value, axes, split_axis=0, concat_axis=0, tiled=True)]
    ppermute x12, waiting for transfers between devices: 49 us -> 40.4 us  [trade_times(): moved[q] = lax.ppermute(blocks[q], 'tm', [(i, i ^ q) for i in range(times)])]
    ppermute x21 -> x27, starting transfers between devices: 15.2 us -> 23.6 us  [swap(): return lax.ppermute(value, 'sl', [(i, i ^ bit) for i in range(SLICES)])]
    ppermute x3, waiting for transfers between devices: 26.1 us -> 31.7 us  [from_group(): return lax.ppermute(value, 'eg', [(i, i ^ f) for i in range(groups)])]
    pallas_call x24 -> x28, Pallas kernels: 107 us -> 112 us  [call(): return pl.pallas_call(kernel, out_shape=out_shape, **options)(*args)]
    ppermute x3, starting transfers between devices: 7.4 us -> 2.68 us  [from_group(): return lax.ppermute(value, 'eg', [(i, i ^ f) for i in range(groups)])]
    ppermute x7 -> x14, starting transfers between devices: 8.05 us -> 11.9 us  [trade(): lax.ppermute(blocks[k], ('tm', 'eg'), [(i, i ^ k) for i in range(count)])]
  transfers between devices with their start and end apart: 46 -> 59, of which waited for: 21 -> 27; matrix products, arithmetic and copies ran while one was open for 1% -> 1% of each run, Pallas kernels for 26% -> 29%
where the time goes in v1:
time: 355 us; the launch traced here: 354 us
  waiting for transfers between devices  146 us (41%)
  Pallas kernels  112 us (32%)
  starting transfers between devices  61.7 us (17%)
  blocking collectives  19.4 us (5%)
  local copies, waits for them, and re-layouts  11.3 us (3%)
    pallas_call x28, Pallas kernels, call(): return pl.pallas_call(kernel, out_shape=out_shape, **options)(*args)  112 us
    ppermute x27, waiting for transfers between devices, swap(): return lax.ppermute(value, 'sl', [(i, i ^ bit) for i in range(SLICES)])  44.7 us
    ppermute x12, waiting for transfers between devices, trade_times(): moved[q] = lax.ppermute(blocks[q], 'tm', [(i, i ^ q) for i in range(times)])  40.4 us
    ppermute x3, waiting for transfers between devices, from_group(): return lax.ppermute(value, 'eg', [(i, i ^ f) for i in range(groups)])  31.7 us
    ppermute x14, waiting for transfers between devices, trade(): lax.ppermute(blocks[k], ('tm', 'eg'), [(i, i ^ k) for i in range(count)])  27.9 us
    ppermute x27, starting transfers between devices, swap(): return lax.ppermute(value, 'sl', [(i, i ^ bit) for i in range(SLICES)])  23.6 us
    all_to_all x1, blocking collectives, exchange(): return lax.all_to_all(value, axes, split_axis=0, concat_axis=0, tiled=True)  19.4 us
    all_to_all x3, starting transfers between devices, exchange(): return lax.all_to_all(value, axes, split_axis=0, concat_axis=0, tiled=True)  14.1 us
  transfers between devices with their start and end apart: 59, of which 27 were waited for; matrix products, arithmetic and copies ran while one was open for 1% of the time, Pallas kernels for 29%

profile of v1, /device:TPU:0, one launch (start us, length us, event | category | flops | bytes accessed | tf_op | source)
XLA Modules:
  0.0 354.1 jit_solution(7250047064974070394)
XLA Ops:
  3.1 7.3 %all-to-all-start = ((bf16[32,64,128]{2,1,0:T(8,128)(2,1)}), bf16[32,64,128]{2,1,0:T(8,128)(2,1)S(1)}, u32[]{:S(2)}, u32[]{:S(2)}) async-start(bf16[32,64,128]{2,1,0:T(8,128)(2,1)} %bitcast.46), calls=%async_computation | async-start | bytes 1048576 | tf_op jit(solution)/shard_map/all_to_all | solution.py:47
  21.1 4.5 %collective-permute-done.18 = f32[8,128]{1,0:T(8,128)S(1)} collective-permute-done((f32[8,128]{1,0:T(8,128)S(1)}, f32[8,128]{1,0:T(8,128)S(1)}, u32[]{:S(2)}, u32[]{:S(2)}) %collective-permute-start.18) | collective-permute-done | bytes 4128 | tf_op jit(solution)/shard_map/ppermute | solution.py:326
  27.8 4.0 %all-to-all-start.1 = ((bf16[32,64,128]{2,1,0:T(8,128)(2,1)}), bf16[32,64,128]{2,1,0:T(8,128)(2,1)S(1)}, u32[]{:S(2)}, u32[]{:S(2)}) async-start(bf16[32,64,128]{2,1,0:T(8,128)(2,1)} %bitcast.6), calls=%async_computation.1 | async-start | bytes 1048576 | tf_op jit(solution)/shard_map/all_to_all | solution.py:47
  32.5 25.5 %collective-permute-done.25.refs_1_ = bf16[128,2048]{1,0:T(8,128)(2,1)S(1)} collective-permute-done((bf16[128,2048]{1,0:T(8,128)(2,1)S(1)}, bf16[128,2048]{1,0:T(8,128)(2,1)S(1)}, u32[]{:S(2)}, u32[]{:S(2)}) %collective-permute-start.25) | collective-permute-done | bytes 524320 | tf_op jit(solution)/shard_map/ppermute | solution.py:326
  77.6 9.9 %collective-permute-done.11.refs_7_ = bf16[128,2048]{1,0:T(8,128)(2,1)} collective-permute-done((bf16[128,2048]{1,0:T(8,128)(2,1)S(1)}, bf16[128,2048]{1,0:T(8,128)(2,1)}, u32[]{:S(2)}, u32[]{:S(2)}) %collective-permute-start.11) | collective-permute-done | bytes 524320 | tf_op jit(solution)/shard_map/ppermute | solution.py:43
  87.5 4.6 %shard_map.139 = (bf16[192,2048]{1,0:T(8,128)(2,1)}, bf16[192,2048]{1,0:T(8,128)(2,1)}, bf16[192,2048]{1,0:T(8,128)(2,1)}, bf16[192,2048]{1,0:T(8,128)(2,1)}) custom-call(f32[8,128]{1,0:T(8,128)} %get-tuple-element.137.refs_0_, f32[8,128]{1,0:T(8,128)} %get-tuple-element.141.refs_1_, f32[8,128]{1,0:T(8,128)} %get-tuple-element.142.refs_2_, ...), custom_call_target="tpu_custom_call" | custom-call | tf_op jit(solution)/shard_map/pallas_call | solution.py:31
  101.6 3.5 %collective-permute-done.21.refs_2_ = bf16[48,2048]{1,0:T(8,128)(2,1)S(1)} collective-permute-done((bf16[48,2048]{1,0:T(8,128)(2,1)}, bf16[48,2048]{1,0:T(8,128)(2,1)S(1)}, u32[]{:S(2)}, u32[]{:S(2)}) %collective-permute-start.21) | collective-permute-done | bytes 196640 | tf_op jit(solution)/shard_map/ppermute | solution.py:336
  113.6 12.7 %collective-permute-done.5.refs_7_ = bf16[128,2048]{1,0:T(8,128)(2,1)} collective-permute-done((bf16[128,2048]{1,0:T(8,128)(2,1)}, bf16[128,2048]{1,0:T(8,128)(2,1)}, u32[]{:S(2)}, u32[]{:S(2)}) %collective-permute-start.5) | collective-permute-done | bytes 524320 | tf_op jit(solution)/shard_map/ppermute | solution.py:43
  126.4 4.1 %shard_map.138 = (bf16[192,2048]{1,0:T(8,128)(2,1)}, bf16[192,2048]{1,0:T(8,128)(2,1)}, bf16[192,2048]{1,0:T(8,128)(2,1)}, bf16[192,2048]{1,0:T(8,128)(2,1)}) custom-call(f32[8,128]{1,0:T(8,128)} %get-tuple-element.137.refs_0_, f32[8,128]{1,0:T(8,128)} %get-tuple-element.141.refs_1_, f32[8,128]{1,0:T(8,128)} %get-tuple-element.142.refs_2_, ...), custom_call_target="tpu_custom_call" | custom-call | tf_op jit(solution)/shard_map/pallas_call | solution.py:31
  134.2 8.9 %collective-permute-done.14.refs_3_ = bf16[192,2048]{1,0:T(8,128)(2,1)} collective-permute-done((bf16[192,2048]{1,0:T(8,128)(2,1)}, bf16[192,2048]{1,0:T(8,128)(2,1)}, u32[]{:S(2)}, u32[]{:S(2)}) %collective-permute-start.14) | collective-permute-done | bytes 786464 | tf_op jit(solution)/shard_map/ppermute | solution.py:336
  147.4 12.5 %collective-permute-done.7.refs_2_ = bf16[192,2048]{1,0:T(8,128)(2,1)S(1)} collective-permute-done((bf16[192,2048]{1,0:T(8,128)(2,1)}, bf16[192,2048]{1,0:T(8,128)(2,1)S(1)}, u32[]{:S(2)}, u32[]{:S(2)}) %collective-permute-start.7) | collective-permute-done | bytes 786464 | tf_op jit(solution)/shard_map/ppermute | solution.py:336
  162.2 5.5 %shard_map.140.refs_4_ = f32[768,512]{1,0:T(8,128)} custom-call(bf16[192,2048]{1,0:T(8,128)(2,1)} %get-tuple-element.71.refs_0_, bf16[192,2048]{1,0:T(8,128)(2,1)} %copy-done.6, bf16[192,2048]{1,0:T(8,128)(2,1)} %collective-permute-done.13.refs_2_, bf16[192,2048]{1,0:T(8,128)(2,1)} %collective-permute-done.14.refs_3_, bf16[512,2048]{1,0:T(8,128)(2,1)} %bitcast.34), custom_call_target="tpu_custom_call" | custom-call | tf_op jit(solution)/shard_map/pallas_call | solution.py:31
  167.8 8.8 %collective-permute-done.8.refs_3_ = bf16[192,2048]{1,0:T(8,128)(2,1)} collective-permute-done((bf16[192,2048]{1,0:T(8,128)(2,1)}, bf16[192,2048]{1,0:T(8,128)(2,1)}, u32[]{:S(2)}, u32[]{:S(2)}) %collective-permute-start.8) | collective-permute-done | bytes 786464 | tf_op jit(solution)/shard_map/ppermute | solution.py:336
  176.5 11.7 %shard_map.141 = (bf16[768,512]{1,0:T(8,128)(2,1)}, bf16[768,512]{1,0:T(8,128)(2,1)}, bf16[768,512]{1,0:T(8,128)(2,1)}, bf16[192,1024]{1,0:T(8,128)(2,1)}, bf16[...) custom-call(bf16[192,2048]{1,0:T(8,128)(2,1)} %get-tuple-element.67., ...), custom_call_target="tpu_custom_call" | custom-call | tf_op jit(solution)/shard_map/pallas_call | solution.py:31
  188.9 3.6 %shard_map.150.refs_1_ = f32[192,512]{1,0:T(8,128)} custom-call(bf16[192,2048]{1,0:T(8,128)(2,1)} %collective-permute-done.33.refs_0_.refs_7_, bf16[512,2048]{1,0:T(8,128)(2,1)} %bitcast.35), custom_call_target="tpu_custom_call" | custom-call | tf_op jit(solution)/shard_map/pallas_call | solution.py:31
  194.5 5.8 %shard_map.151 = (bf16[192,512]{1,0:T(8,128)(2,1)}, bf16[192,512]{1,0:T(8,128)(2,1)}, bf16[192,512]{1,0:T(8,128)(2,1)}, bf16[192,1024]{1,0:T(8,128)(2,1)}, bf16[192,1024]{1,0:T(8,128)(2,1)}) custom-call(bf16[192,2048]{1,0:T(8,128)(2,1)} %collective-permute-done.32.refs_0_.refs_7_, f32[192,512]{1,0:T(8,128)} %shard_map.150.refs_1_, ...), custom_call_target="tpu_custom_call" | custom-call | tf_op jit(solution)/shard_map/pallas_call | solution.py:31
  206.5 4.7 %shard_map.148.refs_3_ = f32[576,512]{1,0:T(8,128)} custom-call(bf16[192,2048]{1,0:T(8,128)(2,1)} %shard_map.147.refs_0_.refs_4_, bf16[192,2048]{1,0:T(8,128)(2,1)} %copy-done.5, bf16[192,2048]{1,0:T(8,128)(2,1)} %collective-permute-done.30.refs_2_.refs_6_, bf16[512,2048]{1,0:T(8,128)(2,1)} %bitcast.36), custom_call_target="tpu_custom_call" | custom-call | tf_op jit(solution)/shard_map/pallas_call | solution.py:31
  213.3 9.6 %shard_map.149 = (bf16[576,512]{1,0:T(8,128)(2,1)}, bf16[576,512]{1,0:T(8,128)(2,1)}, bf16[576,512]{1,0:T(8,128)(2,1)}, bf16[192,1024]{1,0:T(8,128)(2,1)}, bf16[...) custom-call(bf16[192,2048]{1,0:T(8,128)(2,1)} %shard_map.145.refs_0_, ...), custom_call_target="tpu_custom_call" | custom-call | tf_op jit(solution)/shard_map/pallas_call | solution.py:31
  231.9 5.7 %collective-permute-done.17.refs_2_ = bf16[192,1024]{1,0:T(8,128)(2,1)S(1)} collective-permute-done((bf16[192,1024]{1,0:T(8,128)(2,1)}, bf16[192,1024]{1,0:T(8,128)(2,1)S(1)}, u32[]{:S(2)}, u32[]{:S(2)}) %collective-permute-start.17) | collective-permute-done | bytes 393248 | tf_op jit(solution)/shard_map/ppermute | solution.py:43
  243.2 2.9 collective-permute-done.31.refs_1_
  247.1 6.7 %collective-permute-done.46.refs_1_ = bf16[192,1024]{1,0:T(8,128)(2,1)S(1)} collective-permute-done((bf16[192,1024]{1,0:T(8,128)(2,1)}, bf16[192,1024]{1,0:T(8,128)(2,1)S(1)}, u32[]{:S(2)}, u32[]{:S(2)}) %collective-permute-start.46) | collective-permute-done | bytes 393248 | tf_op jit(solution)/shard_map/ppermute | solution.py:43
  265.0 2.9 collective-permute-start.42
  268.6 7.5 %collective-permute-done.36.refs_1_ = bf16[48,1024]{1,0:T(8,128)(2,1)S(1)} collective-permute-done((bf16[48,1024]{1,0:T(8,128)(2,1)}, bf16[48,1024]{1,0:T(8,128)(2,1)S(1)}, u32[]{:S(2)}, u32[]{:S(2)}) %collective-permute-start.36) | collective-permute-done | bytes 98336 | tf_op jit(solution)/shard_map/ppermute | solution.py:54
  278.4 3.8 %collective-permute-done.40.refs_5_ = bf16[48,1024]{1,0:T(8,128)(2,1)S(1)} collective-permute-done((bf16[48,1024]{1,0:T(8,128)(2,1)}, bf16[48,1024]{1,0:T(8,128)(2,1)S(1)}, u32[]{:S(2)}, u32[]{:S(2)}) %collective-permute-start.40) | collective-permute-done | bytes 98336 | tf_op jit(solution)/shard_map/ppermute | solution.py:54
  282.2 4.0 %collective-permute-done.42.refs_7_ = bf16[48,1024]{1,0:T(8,128)(2,1)S(1)} collective-permute-done((bf16[48,1024]{1,0:T(8,128)(2,1)}, bf16[48,1024]{1,0:T(8,128)(2,1)S(1)}, u32[]{:S(2)}, u32[]{:S(2)}) %collective-permute-start.42) | collective-permute-done | bytes 98336 | tf_op jit(solution)/shard_map/ppermute | solution.py:54
  286.3 4.5 %collective-permute-done.49.refs_9_ = bf16[48,1024]{1,0:T(8,128)(2,1)S(1)} collective-permute-done((bf16[48,1024]{1,0:T(8,128)(2,1)}, bf16[48,1024]{1,0:T(8,128)(2,1)S(1)}, u32[]{:S(2)}, u32[]{:S(2)}) %collective-permute-start.49) | collective-permute-done | bytes 98336 | tf_op jit(solution)/shard_map/ppermute | solution.py:54
  297.5 4.0 %shard_map.158 = (bf16[2048,128]{1,0:T(8,128)(2,1)}, bf16[128,2048]{1,0:T(8,128)(2,1)}) custom-call(s32[2,128]{1,0:T(2,128)} %get-tuple-element.128.places, bf16[128,2048]{1,0:T(8,128)(2,1)} %queries.3, bf16[2048,128]{1,0:T(8,128)(2,1)} %bitcast.44, bf16[128,2048]{1,0:T(8,128)(2,1)} %out_grad.1, bf16[48,1024]{1,0:T(8,128)(2,1)} %get-tuple-element.79.refs_0_, ...), custom_call_target="tpu_custom_call" | custom-call | tf_op jit(solution)/shard_map/pallas_call | solution.py:31
  301.5 19.4 %all_to_all.40 = bf16[32,64,128]{2,1,0:T(8,128)(2,1)S(1)} all-to-all(bf16[32,64,128]{2,1,0:T(8,128)(2,1)} %bitcast.48), channel_id=1, replica_groups=mesh['tm'=4,'eg'=2,'sl'=4] {'tm','eg','sl'}, dimensions={0} | all-to-all | bytes 1048576 | tf_op jit(solution)/shard_map/all_to_all | solution.py:47
  324.8 7.7 %shard_map.161 = f32[1,2048,512]{2,1,0:T(8,128)} custom-call(bf16[192,2048]{1,0:T(8,128)(2,1)} %get-tuple-element.67.refs_0_, bf16[192,2048]{1,0:T(8,128)(2,1)} %copy-done.3, bf16[192,2048]{1,0:T(8,128)(2,1)} %copy-done.4, bf16[192,2048]{1,0:T(8,128)(2,1)} %collective-permute-done.8.refs_3_, bf16[192,2048]{1,0:T(8,128)(2,1)} %shard_map.145.refs_0_.refs_4_, ...), custom_call_target="tpu_custom_call" | custom-call | tf_op jit(solution)/shard_map/pallas_call | solution.py:31
  332.5 7.7 %shard_map.162 = f32[1,2048,512]{2,1,0:T(8,128)} custom-call(bf16[192,2048]{1,0:T(8,128)(2,1)} %get-tuple-element.67.refs_0_, bf16[192,2048]{1,0:T(8,128)(2,1)} %copy-done.3, bf16[192,2048]{1,0:T(8,128)(2,1)} %copy-done.4, bf16[192,2048]{1,0:T(8,128)(2,1)} %collective-permute-done.8.refs_3_, bf16[192,2048]{1,0:T(8,128)(2,1)} %shard_map.145.refs_0_.refs_4_, ...), custom_call_target="tpu_custom_call" | custom-call | tf_op jit(solution)/shard_map/pallas_call | solution.py:31
  340.1 7.7 %shard_map.163 = f32[1,512,2048]{2,1,0:T(8,128)} custom-call(bf16[192,2048]{1,0:T(8,128)(2,1)} %get-tuple-element.71.refs_0_, bf16[192,2048]{1,0:T(8,128)(2,1)} %copy-done.6, bf16[192,2048]{1,0:T(8,128)(2,1)} %collective-permute-done.13.refs_2_, bf16[192,2048]{1,0:T(8,128)(2,1)} %collective-permute-done.14.refs_3_, ...), custom_call_target="tpu_custom_call" | custom-call | tf_op jit(solution)/shard_map/pallas_call | solution.py:31
  351.2 2.9 shard_map.160
  (252 shorter events, 118.1 us)
Async XLA Ops:
  3.1 23.7 %all-to-all-start = ((bf16[32,64,128]{2,1,0:T(8,128)(2,1)}), bf16[32,64,128]{2,1,0:T(8,128)(2,1)S(1)}, u32[]{:S(2)}, u32[]{:S(2)}) async-start(bf16[32,64,128]{2,1,0:T(8,128)(2,1)} %bitcast.46), calls=%async_computation | async-start | bytes 1048576 | tf_op jit(solution)/shard_map/all_to_all | solution.py:47
  19.5 44.8 %collective-permute-start.10 = (bf16[128,2048]{1,0:T(8,128)(2,1)S(1)}, bf16[128,2048]{1,0:T(8,128)(2,1)S(1)}, u32[]{:S(2)}, u32[]{:S(2)}) collective-permute-start(bf16[128,2048]{1,0:T(8,128)(2,1)S(1)} %copy-done.8), channel_id=1, source_target_pairs={{0,2},{1,3},{2,0},{3,1},{4,6},{5,7},{6,4},{7,5},{8,10},{9,11},{10,... | collective-permute-start | bytes 1572872 | tf_op jit(solution)/shard_map/ppermute | solution.py:43
  25.5 32.5 %collective-permute-start.25 = (bf16[128,2048]{1,0:T(8,128)(2,1)S(1)}, bf16[128,2048]{1,0:T(8,128)(2,1)S(1)}, u32[]{:S(2)}, u32[]{:S(2)}) collective-permute-start(bf16[128,2048]{1,0:T(8,128)(2,1)S(1)} %copy-done.8), channel_id=1, source_target_pairs={{0,4},{4,0},{1,5},{5,1},{2,6},{6,2},{3,7},{7,3},{8,12},{12,8},{9,1... | collective-permute-start | bytes 1572872 | tf_op jit(solution)/shard_map/ppermute | solution.py:326
  27.8 37.1 %all-to-all-start.1 = ((bf16[32,64,128]{2,1,0:T(8,128)(2,1)}), bf16[32,64,128]{2,1,0:T(8,128)(2,1)S(1)}, u32[]{:S(2)}, u32[]{:S(2)}) async-start(bf16[32,64,128]{2,1,0:T(8,128)(2,1)} %bitcast.6), calls=%async_computation.1 | async-start | bytes 1048576 | tf_op jit(solution)/shard_map/all_to_all | solution.py:47
  64.3 23.2 %collective-permute-start.11 = (bf16[128,2048]{1,0:T(8,128)(2,1)S(1)}, bf16[128,2048]{1,0:T(8,128)(2,1)}, u32[]{:S(2)}, u32[]{:S(2)}) collective-permute-start(bf16[128,2048]{1,0:T(8,128)(2,1)S(1)} %collective-permute-done.10.refs_6_), channel_id=1, source_target_pairs={{0,1},{1,0},{2,3},{3,2},{4,5},{5,4},{6,7},{7,6},{8,9},{9,8},{10,11... | collective-permute-start | bytes 1572872 | tf_op jit(solution)/shard_map/ppermute | solution.py:43
  68.2 25.6 %collective-permute-start.19 = (bf16[128,2048]{1,0:T(8,128)(2,1)}, bf16[128,2048]{1,0:T(8,128)(2,1)S(1)}, u32[]{:S(2)}, u32[]{:S(2)}) collective-permute-start(bf16[128,2048]{1,0:T(8,128)(2,1)} %shard_map.137.refs_4_), channel_id=1, source_target_pairs={{0,4},{4,0},{1,5},{5,1},{2,6},{6,2},{3,7},{7,3},{8,12},{12,8},{9,1... | collective-permute-start | bytes 1572872 | tf_op jit(solution)/shard_map/ppermute | solution.py:326
  70.8 27.8 %collective-permute-start.3 = (bf16[128,2048]{1,0:T(8,128)(2,1)}, bf16[128,2048]{1,0:T(8,128)(2,1)S(1)}, u32[]{:S(2)}, u32[]{:S(2)}) collective-permute-start(bf16[128,2048]{1,0:T(8,128)(2,1)} %shard_map.137.refs_4_), channel_id=1, source_target_pairs={{0,1},{1,0},{2,3},{3,2},{4,5},{5,4},{6,7},{7,6},{8,9},{9,8},{10,11... | collective-permute-start | bytes 1572872 | tf_op jit(solution)/shard_map/ppermute | solution.py:43
  73.5 26.6 %collective-permute-start.4 = (bf16[128,2048]{1,0:T(8,128)(2,1)}, bf16[128,2048]{1,0:T(8,128)(2,1)}, u32[]{:S(2)}, u32[]{:S(2)}) collective-permute-start(bf16[128,2048]{1,0:T(8,128)(2,1)} %shard_map.137.refs_4_), channel_id=1, source_target_pairs={{0,2},{1,3},{2,0},{3,1},{4,6},{5,7},{6,4},{7,5},{8,10},{9,11},{10,... | collective-permute-start | bytes 1572872 | tf_op jit(solution)/shard_map/ppermute | solution.py:43
  76.4 54.1 %collective-permute-start.29 = (bf16[192,2048]{1,0:T(8,128)(2,1)}, bf16[192,2048]{1,0:T(8,128)(2,1)S(1)}, u32[]{:S(2)}, u32[]{:S(2)}) collective-permute-start(bf16[192,2048]{1,0:T(8,128)(2,1)} %shard_map.147.refs_0_.refs_4_), channel_id=1, source_target_pairs={{0,1},{1,0},{2,3},{3,2},{4,5},{5,4},{6,7},{7,6},{8,9},{9,8},{10,11... | collective-permute-start | bytes 2359304 | tf_op jit(solution)/shard_map/ppermute | solution.py:43
  92.1 39.3 %collective-permute-start.12 = (bf16[192,2048]{1,0:T(8,128)(2,1)}, bf16[192,2048]{1,0:T(8,128)(2,1)S(1)}, u32[]{:S(2)}, u32[]{:S(2)}) collective-permute-start(bf16[192,2048]{1,0:T(8,128)(2,1)} %get-tuple-element.72), channel_id=1, source_target_pairs={{0,8},{8,0},{16,24},{24,16},{1,9},{9,1},{17,25},{25,17},{2,10},{10... | collective-permute-start | bytes 2359304 | tf_op jit(solution)/shard_map/ppermute | solution.py:336
  100.1 26.2 %collective-permute-start.5 = (bf16[128,2048]{1,0:T(8,128)(2,1)}, bf16[128,2048]{1,0:T(8,128)(2,1)}, u32[]{:S(2)}, u32[]{:S(2)}) collective-permute-start(bf16[128,2048]{1,0:T(8,128)(2,1)} %collective-permute-done.4.refs_6_), channel_id=1, source_target_pairs={{0,1},{1,0},{2,3},{3,2},{4,5},{5,4},{6,7},{7,6},{8,9},{9,8},{10,11... | collective-permute-start | bytes 1572872 | tf_op jit(solution)/shard_map/ppermute | solution.py:43
  105.2 28.6 %collective-permute-start.13 = (bf16[192,2048]{1,0:T(8,128)(2,1)}, bf16[192,2048]{1,0:T(8,128)(2,1)}, u32[]{:S(2)}, u32[]{:S(2)}) collective-permute-start(bf16[192,2048]{1,0:T(8,128)(2,1)} %get-tuple-element.73), channel_id=1, source_target_pairs={{0,16},{8,24},{16,0},{24,8},{1,17},{9,25},{17,1},{25,9},{2,18},{10... | collective-permute-start | bytes 2359304 | tf_op jit(solution)/shard_map/ppermute | solution.py:336
  109.4 33.7 %collective-permute-start.14 = (bf16[192,2048]{1,0:T(8,128)(2,1)}, bf16[192,2048]{1,0:T(8,128)(2,1)}, u32[]{:S(2)}, u32[]{:S(2)}) collective-permute-start(bf16[192,2048]{1,0:T(8,128)(2,1)} %get-tuple-element.74), channel_id=1, source_target_pairs={{0,24},{8,16},{16,8},{24,0},{1,25},{9,17},{17,9},{25,1},{2,26},{10... | collective-permute-start | bytes 2359304 | tf_op jit(solution)/shard_map/ppermute | solution.py:336
  132.3 27.6 %collective-permute-start.7 = (bf16[192,2048]{1,0:T(8,128)(2,1)}, bf16[192,2048]{1,0:T(8,128)(2,1)S(1)}, u32[]{:S(2)}, u32[]{:S(2)}) collective-permute-start(bf16[192,2048]{1,0:T(8,128)(2,1)} %get-tuple-element.69), channel_id=1, source_target_pairs={{0,16},{8,24},{16,0},{24,8},{1,17},{9,25},{17,1},{25,9},{2,18},{10... | collective-permute-start | bytes 2359304 | tf_op jit(solution)/shard_map/ppermute | solution.py:336
  133.8 42.8 %collective-permute-start.8 = (bf16[192,2048]{1,0:T(8,128)(2,1)}, bf16[192,2048]{1,0:T(8,128)(2,1)}, u32[]{:S(2)}, u32[]{:S(2)}) collective-permute-start(bf16[192,2048]{1,0:T(8,128)(2,1)} %get-tuple-element.70), channel_id=1, source_target_pairs={{0,24},{8,16},{16,8},{24,0},{1,25},{9,17},{17,9},{25,1},{2,26},{10... | collective-permute-start | bytes 2359304 | tf_op jit(solution)/shard_map/ppermute | solution.py:336
  143.1 45.1 %collective-permute-start.33 = (bf16[192,2048]{1,0:T(8,128)(2,1)}, bf16[192,2048]{1,0:T(8,128)(2,1)}, u32[]{:S(2)}, u32[]{:S(2)}) collective-permute-start(bf16[192,2048]{1,0:T(8,128)(2,1)} %copy-done.5), channel_id=1, source_target_pairs={{0,2},{1,3},{2,0},{3,1},{4,6},{5,7},{6,4},{7,5},{8,10},{9,11},{10,... | collective-permute-start | bytes 2359304 | tf_op jit(solution)/shard_map/ppermute | solution.py:43
  145.7 46.8 %collective-permute-start.32 = (bf16[192,2048]{1,0:T(8,128)(2,1)S(1)}, bf16[192,2048]{1,0:T(8,128)(2,1)}, u32[]{:S(2)}, u32[]{:S(2)}) collective-permute-start(bf16[192,2048]{1,0:T(8,128)(2,1)S(1)} %collective-permute-done.24.refs_2_.refs_6_), channel_id=1, source_target_pairs={{0,1},{1,0},{2,3},{3,2},{4,5},{5,4},{6,7},{7,6},{8,9},{9,8},{10,11... | collective-permute-start | bytes 2359304 | tf_op jit(solution)/shard_map/ppermute | solution.py:43
  147.1 53.2 %collective-permute-start.30 = (bf16[192,2048]{1,0:T(8,128)(2,1)}, bf16[192,2048]{1,0:T(8,128)(2,1)}, u32[]{:S(2)}, u32[]{:S(2)}) collective-permute-start(bf16[192,2048]{1,0:T(8,128)(2,1)} %shard_map.147.refs_0_.refs_4_), channel_id=1, source_target_pairs={{0,2},{1,3},{2,0},{3,1},{4,6},{5,7},{6,4},{7,5},{8,10},{9,11},{10,... | collective-permute-start | bytes 2359304 | tf_op jit(solution)/shard_map/ppermute | solution.py:43
  159.9 41.9 %collective-permute-start.23 = (bf16[192,2048]{1,0:T(8,128)(2,1)S(1)}, bf16[192,2048]{1,0:T(8,128)(2,1)}, u32[]{:S(2)}, u32[]{:S(2)}) collective-permute-start(bf16[192,2048]{1,0:T(8,128)(2,1)S(1)} %copy-done), channel_id=1, source_target_pairs={{0,1},{1,0},{2,3},{3,2},{4,5},{5,4},{6,7},{7,6},{8,9},{9,8},{10,11... | collective-permute-start | bytes 2359304 | tf_op jit(solution)/shard_map/ppermute | solution.py:43
  192.5 20.7 %collective-permute-start.15 = (bf16[192,1024]{1,0:T(8,128)(2,1)S(1)}, bf16[192,1024]{1,0:T(8,128)(2,1)S(1)}, u32[]{:S(2)}, u32[]{:S(2)}) collective-permute-start(bf16[192,1024]{1,0:T(8,128)(2,1)S(1)} %copy-done.49), channel_id=1, source_target_pairs={{0,2},{1,3},{2,0},{3,1},{4,6},{5,7},{6,4},{7,5},{8,10},{9,11},{10,... | collective-permute-start | bytes 1179656 | tf_op jit(solution)/shard_map/ppermute | solution.py:43
  200.3 22.6 %collective-permute-start.43 = (bf16[192,1024]{1,0:T(8,128)(2,1)S(1)}, bf16[192,1024]{1,0:T(8,128)(2,1)S(1)}, u32[]{:S(2)}, u32[]{:S(2)}) collective-permute-start(bf16[192,1024]{1,0:T(8,128)(2,1)S(1)} %copy-done.48), channel_id=1, source_target_pairs={{0,1},{1,0},{2,3},{3,2},{4,5},{5,4},{6,7},{7,6},{8,9},{9,8},{10,11... | collective-permute-start | bytes 1179656 | tf_op jit(solution)/shard_map/ppermute | solution.py:43
  201.8 22.5 %collective-permute-start.34 = (bf16[192,1024]{1,0:T(8,128)(2,1)}, bf16[192,1024]{1,0:T(8,128)(2,1)S(1)}, u32[]{:S(2)}, u32[]{:S(2)}) collective-permute-start(bf16[192,1024]{1,0:T(8,128)(2,1)} %get-tuple-element.91), channel_id=1, source_target_pairs={{0,1},{1,0},{2,3},{3,2},{4,5},{5,4},{6,7},{7,6},{8,9},{9,8},{10,11... | collective-permute-start | bytes 1179656 | tf_op jit(solution)/shard_map/ppermute | solution.py:43
  202.4 26.8 %collective-permute-start.47 = (bf16[192,1024]{1,0:T(8,128)(2,1)}, bf16[192,1024]{1,0:T(8,128)(2,1)S(1)}, u32[]{:S(2)}, u32[]{:S(2)}) collective-permute-start(bf16[192,1024]{1,0:T(8,128)(2,1)} %get-tuple-element.107), channel_id=1, source_target_pairs={{0,1},{1,0},{2,3},{3,2},{4,5},{5,4},{6,7},{7,6},{8,9},{9,8},{10,11... | collective-permute-start | bytes 1179656 | tf_op jit(solution)/shard_map/ppermute | solution.py:43
  205.8 31.9 %collective-permute-start.17 = (bf16[192,1024]{1,0:T(8,128)(2,1)}, bf16[192,1024]{1,0:T(8,128)(2,1)S(1)}, u32[]{:S(2)}, u32[]{:S(2)}) collective-permute-start(bf16[192,1024]{1,0:T(8,128)(2,1)} %shard_map.142), channel_id=1, source_target_pairs={{0,1},{1,0},{2,3},{3,2},{4,5},{5,4},{6,7},{7,6},{8,9},{9,8},{10,11... | collective-permute-start | bytes 1179656 | tf_op jit(solution)/shard_map/ppermute | solution.py:43
  213.2 27.2 %collective-permute-start.45 = (bf16[192,1024]{1,0:T(8,128)(2,1)}, bf16[192,1024]{1,0:T(8,128)(2,1)S(1)}, u32[]{:S(2)}, u32[]{:S(2)}) collective-permute-start(bf16[192,1024]{1,0:T(8,128)(2,1)} %shard_map.154), channel_id=1, source_target_pairs={{0,2},{1,3},{2,0},{3,1},{4,6},{5,7},{6,4},{7,5},{8,10},{9,11},{10,... | collective-permute-start | bytes 1179656 | tf_op jit(solution)/shard_map/ppermute | solution.py:43
  222.9 23.2 %collective-permute-start.31 = (bf16[192,1024]{1,0:T(8,128)(2,1)}, bf16[192,1024]{1,0:T(8,128)(2,1)S(1)}, u32[]{:S(2)}, u32[]{:S(2)}) collective-permute-start(bf16[192,1024]{1,0:T(8,128)(2,1)} %get-tuple-element.89), channel_id=1, source_target_pairs={{0,1},{1,0},{2,3},{3,2},{4,5},{5,4},{6,7},{7,6},{8,9},{9,8},{10,11... | collective-permute-start | bytes 1179656 | tf_op jit(solution)/shard_map/ppermute | solution.py:43
  224.3 29.5 %collective-permute-start.46 = (bf16[192,1024]{1,0:T(8,128)(2,1)}, bf16[192,1024]{1,0:T(8,128)(2,1)S(1)}, u32[]{:S(2)}, u32[]{:S(2)}) collective-permute-start(bf16[192,1024]{1,0:T(8,128)(2,1)} %get-tuple-element.105), channel_id=1, source_target_pairs={{0,1},{1,0},{2,3},{3,2},{4,5},{5,4},{6,7},{7,6},{8,9},{9,8},{10,11... | collective-permute-start | bytes 1179656 | tf_op jit(solution)/shard_map/ppermute | solution.py:43
  229.2 25.6 %collective-permute-start.35 = (bf16[192,1024]{1,0:T(8,128)(2,1)}, bf16[192,1024]{1,0:T(8,128)(2,1)S(1)}, u32[]{:S(2)}, u32[]{:S(2)}) collective-permute-start(bf16[192,1024]{1,0:T(8,128)(2,1)} %shard_map.152), channel_id=1, source_target_pairs={{0,2},{1,3},{2,0},{3,1},{4,6},{5,7},{6,4},{7,5},{8,10},{9,11},{10,... | collective-permute-start | bytes 1179656 | tf_op jit(solution)/shard_map/ppermute | solution.py:43
  237.7 24.4 %collective-permute-start.48 = (bf16[192,1024]{1,0:T(8,128)(2,1)}, bf16[192,1024]{1,0:T(8,128)(2,1)S(1)}, u32[]{:S(2)}, u32[]{:S(2)}) collective-permute-start(bf16[192,1024]{1,0:T(8,128)(2,1)} %shard_map.156), channel_id=1, source_target_pairs={{0,2},{1,3},{2,0},{3,1},{4,6},{5,7},{6,4},{7,5},{8,10},{9,11},{10,... | collective-permute-start | bytes 1179656 | tf_op jit(solution)/shard_map/ppermute | solution.py:43
  265.0 21.3 %collective-permute-start.42 = (bf16[48,1024]{1,0:T(8,128)(2,1)}, bf16[48,1024]{1,0:T(8,128)(2,1)S(1)}, u32[]{:S(2)}, u32[]{:S(2)}) collective-permute-start(bf16[48,1024]{1,0:T(8,128)(2,1)} %get-tuple-element.98), channel_id=1, source_target_pairs={{0,28},{4,24},{8,20},{12,16},{16,12},{20,8},{24,4},{28,0},{1,29},{... | collective-permute-start | bytes 294920 | tf_op jit(solution)/shard_map/ppermute | solution.py:54
  267.9 22.9 %collective-permute-start.49 = (bf16[48,1024]{1,0:T(8,128)(2,1)}, bf16[48,1024]{1,0:T(8,128)(2,1)S(1)}, u32[]{:S(2)}, u32[]{:S(2)}) collective-permute-start(bf16[48,1024]{1,0:T(8,128)(2,1)} %get-tuple-element.108), channel_id=1, source_target_pairs={{0,4},{4,0},{8,12},{12,8},{16,20},{20,16},{24,28},{28,24},{1,5},{5... | collective-permute-start | bytes 294920 | tf_op jit(solution)/shard_map/ppermute | solution.py:54
  321.9 28.4 %all-to-all-start.3 = ((bf16[32,64,128]{2,1,0:T(8,128)(2,1)}), bf16[32,64,128]{2,1,0:T(8,128)(2,1)S(1)}, u32[]{:S(2)}, u32[]{:S(2)}) async-start(bf16[32,64,128]{2,1,0:T(8,128)(2,1)} %bitcast.14), calls=%async_computation.3 | async-start | bytes 1048576 | tf_op jit(solution)/shard_map/all_to_all | solution.py:47
  (77 other events, 918.2 us)
